TPU v7x, 512 devices: a whole 4x8x8 slice. The times are simulated.
512 devices in a mesh: row: 16 (over x, y_lo), col: 32 (over y_hi, z, core).
Axes of the slice: x: 4, y: 8 (y_hi: 2, y_lo: 4; y = y_hi * 4 + y_lo), z: 8, core: 2. Of those that a mesh axis runs over, the one named last changes fastest.
Arguments:
- bricks: bfloat16 [16, 32, 2, 16, 128, 128], P('row', 'col'), may hold values from -393216 to 393216
- brick_coords: int32 [16, 32, 3, 2], P('row', 'col'), may hold values from 0 to 31, as said below
- brick_counts: int32 [16, 32], P('row', 'col'), may hold values from 0 to 2, as said below
- step_sizes: float32 [2, 3], replicated, may hold values from 0.3 to 1
- init_a: float32 [16, 512, 256], P('row', 'col'), may hold values from -6 to 6
- init_b: float32 [32, 256, 256], P('col', 'row'), may hold values from -6 to 6
- init_c: float32 [512, 256], replicated, may hold values from -6 to 6
Outputs:
- factor_a: float32 [16, 512, 256], P('row', 'col')
- factor_b: float32 [32, 256, 256], P('col', 'row')
- factor_c: float32 [512, 256], replicated
Inputs may be any that keep to these rules, and one draw needn't show every extreme that they name: brick_counts of rows r and (r + half of the row axis) mod the row axis in one column add up to at most 3; some device holds 2 bricks. `brick_coords`: component 0 is below 4, component 1 below 2, component 2 below 32; dead slots hold arbitrary positions.
All inputs are finite; a program needn't handle non-finite values.
Results may differ from a plain program's by a relative error of at most 0.0003.
The roundings to bfloat16 on the way count: a program that leaves them out, or rounds other values in their place, can miss the bound.
Values may be sent and summed in bfloat16 or wider, within the bound.
No kernel may reach another device: no remote copies, remote signals or barrier semaphores. Data moves between devices by JAX's collectives and lax.ppermute only.
A program may use at most 64 MiB of HBM per device.

v0:
```python
import jax
import jax.numpy as jnp
from jax import lax
from jax.sharding import PartitionSpec as P


def brick_terms(brick, a_tile, b_tile, c_rows):
    depth, tile, _ = brick.shape
    wide = jnp.dot(
        brick.reshape(depth * tile, tile), b_tile, preferred_element_type=jnp.float32
    ).reshape(depth, tile, -1)
    c_wide = c_rows.astype(jnp.float32)[:, None, :]
    along_a = jnp.sum(wide * c_wide, axis=0)
    deep = jnp.einsum("kij,ir->kjr", brick, a_tile, preferred_element_type=jnp.float32)
    along_b = jnp.sum(deep * c_wide, axis=0)
    along_c = jnp.sum(deep * b_tile.astype(jnp.float32)[None, :, :], axis=1)
    return (along_a, along_b, along_c)


def add_tile(total, delta, start):
    old = lax.dynamic_slice_in_dim(total, start, delta.shape[0], 0)
    return lax.dynamic_update_slice_in_dim(total, old + delta, start, 0)


def gram(values):
    return jnp.dot(values.T, values, preferred_element_type=jnp.float32)


def project(state, hess, drive, rate):
    scale = jnp.sum(jnp.abs(hess), axis=1) + 1e-06
    slope = (
        jnp.dot(state, hess, precision=lax.Precision.HIGHEST, preferred_element_type=jnp.float32)
        - drive
    )
    return jnp.maximum(state - rate * slope / scale[None, :], 0.0)


def shards(bricks, brick_coords, brick_counts, step_sizes, init_a, init_b, init_c):
    slab = bricks[0, 0]
    places = brick_coords[0, 0]
    own = brick_counts[0, 0]
    depth = slab.shape[1]
    tile = slab.shape[2]
    sweeps = step_sizes.shape[0]
    state_a = init_a[0]
    state_b = init_b[0]
    state_c = init_c
    for sweep in range(sweeps):
        a_bf = state_a.astype(jnp.bfloat16)
        b_bf = state_b.astype(jnp.bfloat16)
        c_bf = state_c.astype(jnp.bfloat16)
        a_range = lax.all_gather(a_bf, "col", axis=0, tiled=True)
        b_range = lax.all_gather(b_bf, "row", axis=0, tiled=True)
        local_ga = gram(a_bf)
        local_gb = gram(b_bf)
        gram_a, gram_b = lax.psum((local_ga, local_gb), ("row", "col"))
        gram_c = gram(c_bf)

        def own_step(slot, carry):
            total_a, total_b, total_c = carry
            brick = lax.dynamic_index_in_dim(slab, slot, 0, keepdims=False)
            spot = lax.dynamic_index_in_dim(places, slot, 1, keepdims=False)
            i_low = spot[0] * tile
            j_low = spot[1] * tile
            k_low = spot[2] * depth
            a_tile = lax.dynamic_slice_in_dim(a_range, i_low, tile, 0)
            b_tile = lax.dynamic_slice_in_dim(b_range, j_low, tile, 0)
            c_rows = lax.dynamic_slice_in_dim(c_bf, k_low, depth, 0)
            delta_a, delta_b, delta_c = brick_terms(brick, a_tile, b_tile, c_rows)
            return (
                add_tile(total_a, delta_a, i_low),
                add_tile(total_b, delta_b, j_low),
                add_tile(total_c, delta_c, k_low),
            )

        empty = (
            jnp.zeros(a_range.shape, jnp.float32),
            jnp.zeros(b_range.shape, jnp.float32),
            jnp.zeros(c_bf.shape, jnp.float32),
        )
        drive_a, drive_b, drive_c = lax.fori_loop(0, own, own_step, empty)
        mine_a = lax.psum_scatter(drive_a, "col", scatter_dimension=0, tiled=True)
        mine_b = lax.psum_scatter(drive_b, "row", scatter_dimension=0, tiled=True)
        summed_c = lax.psum(drive_c, ("row", "col"))
        new_c = project(state_c, gram_a * gram_b, summed_c, step_sizes[sweep, 2])
        new_a = project(state_a, gram_b * gram_c, mine_a, step_sizes[sweep, 0])
        new_b = project(state_b, gram_a * gram_c, mine_b, step_sizes[sweep, 1])
        state_a, state_b, state_c = (new_a, new_b, new_c)
    return (state_a[None], state_b[None], state_c)


def solution(mesh):
    placed = (
        P("row", "col", None, None, None, None),
        P("row", "col", None, None),
        P("row", "col"),
        P(),
        P("row", "col", None),
        P("col", "row", None),
        P(),
    )
    return jax.shard_map(
        shards,
        mesh=mesh,
        in_specs=placed,
        out_specs=(P("row", "col", None), P("col", "row", None), P()),
        check_vma=False,
    )
```

profile of v0, /device:TPU:17, one launch (start us, length us, event | category | flops | bytes accessed | tf_op | source)
XLA Modules:
  0.0 791.6 jit_solution(12172388770690643116)
XLA Ops:
  8.1 1.7 fusion.61
  9.8 0.7 bitcast_convert_fusion
  10.5 1.7 fusion.59
  12.2 0.7 bitcast_convert_fusion.1
  13.0 31.3 %all_gather.12 = bf16[256,256]{1,0:T(8,128)(2,1)S(1)} all-gather(bf16[16,256]{1,0:T(8,128)(2,1)S(1)} %bitcast_convert_fusion), channel_id=1, replica_groups=mesh['row'=16,'col'=32] {'row'}, dimensions={0}, use_global_device_ids=true | all-gather | bytes 139264 | tf_op jit(solution)/shard_map/all_gather | solution.py:53
  44.3 65.9 %all_gather.13 = bf16[512,256]{1,0:T(8,128)(2,1)S(1)} all-gather(bf16[16,256]{1,0:T(8,128)(2,1)S(1)} %bitcast_convert_fusion.1), channel_id=1, replica_groups=mesh['row'=16,'col'=32] {'col'}, dimensions={0}, use_global_device_ids=true | all-gather | bytes 270336 | tf_op jit(solution)/shard_map/all_gather | solution.py:52
  110.4 6.1 while.28
  111.0 0.6 fusion.93
  113.6 1.7 multiply_reduce_fusion.10
  116.5 1.0 copy.16
  118.2 0.5 reduce-scatter.5.cloned.1.call-update
  119.0 0.7 fusion.67
  119.6 275.4 %all-reduce.7.cloned.1.call-done = (f32[256,256]{1,0:T(8,128)}, f32[256,256]{1,0:T(8,128)}, f32[512,256]{0,1:T(8,128)}) async-done(((f32[256,256]{1,0:T(8,128)}, f32[256,256]{1,0:T(8,128)}, f32[512,256]{0,1:T(8,128)}), (f32[256,256]{1,0:T(8,128)}, f32[256,256]{1,0:T(8,128)}, f32[512,256]{0,1:T(8,128)})) %all-reduce.7.cloned.1.call-update) | async-done | bytes 1048592 | tf_op jit(solution)/shard_map/psum | solution.py:56
  395.1 1.5 abs_reduce_fusion.3
  396.6 1.7 fusion.69
  398.6 1.6 fusion.68
  400.2 29.4 %all_gather.14 = bf16[256,256]{1,0:T(8,128)(2,1)S(1)} all-gather(bf16[16,256]{1,0:T(8,128)(2,1)S(1)} %get-tuple-element.215), channel_id=1, replica_groups=mesh['row'=16,'col'=32] {'row'}, dimensions={0}, use_global_device_ids=true | all-gather | bytes 139264 | tf_op jit(solution)/shard_map/all_gather | solution.py:53
  429.6 0.9 fusion.71
  430.5 1.6 fusion.70
  432.1 56.0 %all_gather.15 = bf16[512,256]{1,0:T(8,128)(2,1)S(1)} all-gather(bf16[16,256]{1,0:T(8,128)(2,1)S(1)} %get-tuple-element.219), channel_id=1, replica_groups=mesh['row'=16,'col'=32] {'col'}, dimensions={0}, use_global_device_ids=true | all-gather | bytes 270336 | tf_op jit(solution)/shard_map/all_gather | solution.py:52
  488.1 1.0 fusion.72
  489.2 6.2 while.29
  489.9 0.7 fusion.96
  492.5 1.7 multiply_reduce_fusion.12
  495.4 1.0 copy.23
  497.1 0.7 reduce-scatter.9.cloned.1.call-update
  497.8 277.9 %all-reduce.5.cloned.1.call-done = (f32[256,256]{1,0:T(8,128)}, f32[256,256]{1,0:T(8,128)}, f32[512,256]{0,1:T(8,128)}) async-done(((f32[256,256]{1,0:T(8,128)}, f32[256,256]{1,0:T(8,128)}, f32[512,256]{0,1:T(8,128)}), (f32[256,256]{1,0:T(8,128)}, f32[256,256]{1,0:T(8,128)}, f32[512,256]{0,1:T(8,128)})) %all-reduce.5.cloned.1.call-update) | async-done | bytes 1048592 | tf_op jit(solution)/shard_map/psum | solution.py:56
  775.7 1.5 abs_reduce_fusion
  777.3 1.4 fusion.30
  778.7 1.0 copy.25
  779.7 2.2 fusion.35
  781.9 2.1 fusion.40
  (74 shorter events, 3.1 us)
Async XLA Ops:
  8.0 36.3 %copy-start.4 = (f32[512,256]{1,0:T(8,128)S(1)}, f32[512,256]{1,0:T(8,128)}, u32[]{:S(2)}) copy-start(f32[512,256]{1,0:T(8,128)} %param.17) | copy-start | bytes 1572868
  8.0 387.1 %all-reduce.7.cloned.1.call-start = ((), (), s32[]{:S(2)}) async-start(), calls=%async_computation.9 | async-start | bytes 2097152 | tf_op jit(solution)/shard_map/psum | solution.py:56
  44.3 66.1 %copy-start.16 = (s32[1,1,3,2]{2,3,1,0:T(2,128)S(1)}, s32[1,1,3,2]{2,3,1,0:T(2,128)}, u32[]{:S(2)}) copy-start(s32[1,1,3,2]{2,3,1,0:T(2,128)} %param.12) | copy-start | bytes 76
  113.5 1.7 copy-start.13
  116.4 1.1 copy-start.1
  116.4 1.1 copy-start.3
  117.5 1.4 copy-start.12
  117.5 281.0 %reduce-scatter.7.cloned.1.call-start = ((), (), s32[]{:S(2)}) async-start(), calls=%async_computation.5 | async-start | bytes 278528 | tf_op jit(solution)/shard_map/reduce_scatter | solution.py:83
  118.1 312.4 %reduce-scatter.5.cloned.1.call-start = ((), (), s32[]{:S(2)}) async-start(), calls=%async_computation.4 | async-start | bytes 540672 | tf_op jit(solution)/shard_map/reduce_scatter | solution.py:82
  118.7 657.0 %all-reduce.5.cloned.1.call-start = ((), (), s32[]{:S(2)}) async-start(), calls=%async_computation.8 | async-start | bytes 2097152 | tf_op jit(solution)/shard_map/psum | solution.py:56
  395.1 1.5 copy-start.5
  395.1 1.5 copy-start.6
  395.1 1.5 copy-start.9
  396.6 2.0 copy-start.10
  398.4 32.1 %copy-start.11 = (f32[1,16,256]{2,1,0:T(8,128)S(1)}, f32[1,16,256]{2,1,0:T(8,128)}, u32[]{:S(2)}) copy-start(f32[1,16,256]{2,1,0:T(8,128)} %param.15) | copy-start | bytes 49156
  492.5 1.7 copy-start.14
  495.4 1.1 copy-start
  495.4 1.1 copy-start.2
  496.5 283.2 %reduce-scatter.11.cloned.1.call-start = ((), (), s32[]{:S(2)}) async-start(), calls=%async_computation.7 | async-start | bytes 278528 | tf_op jit(solution)/shard_map/reduce_scatter | solution.py:83
  497.1 284.8 %reduce-scatter.9.cloned.1.call-start = ((), (), s32[]{:S(2)}) async-start(), calls=%async_computation.6 | async-start | bytes 540672 | tf_op jit(solution)/shard_map/reduce_scatter | solution.py:82
  775.7 1.5 copy-start.7
  775.7 1.5 copy-start.8
  775.7 1.5 copy-start.15
Sparse Core Ops, SparseCore 0:
  117.6 277.4 all-reduce.6
  496.6 279.0 all-reduce.4
Sparse Core Ops, SparseCore 1:
  120.8 68.2 reduce-scatter.6
  193.5 133.6 reduce-scatter.4
  499.8 69.9 reduce-scatter.10
  574.3 133.7 reduce-scatter.8
where the time goes:
time: 793 us; the launch traced here: 792 us
  waiting for transfers between devices  556 us (70%)
  blocking collectives  183 us (23%)
  matrix products  23.2 us (3%)
  between operations  16 us (2%)
    psum x2, waiting for transfers between devices, shards(): gram_a, gram_b = lax.psum((local_ga, local_gb), ('row', 'col'))  553 us
    all_gather x2, blocking collectives, shards(): a_range = lax.all_gather(a_bf, 'col', axis=0, tiled=True)  122 us
    all_gather x2, blocking collectives, shards(): b_range = lax.all_gather(b_bf, 'row', axis=0, tiled=True)  60.7 us
  transfers between devices with their start and end apart: 6, of which 2 were waited for; matrix products, arithmetic and copies ran while one was open for 2% of the time, Pallas kernels for 0%

commit v1 on v0

--- a/solution.py
+++ b/solution.py
@@ -50,7 +50,11 @@
         b_bf = state_b.astype(jnp.bfloat16)
         c_bf = state_c.astype(jnp.bfloat16)
         a_range = lax.all_gather(a_bf, "col", axis=0, tiled=True)
-        b_range = lax.all_gather(b_bf, "row", axis=0, tiled=True)
+        tracks_supply = lambda mat, mesh_dim: jnp.concatenate(
+            lax.all_to_all(jnp.stack([mat] * lax.axis_size(mesh_dim), axis=0), mesh_dim, 0, 0),
+            axis=0,
+        )
+        b_range = tracks_supply(b_bf, "row")
         local_ga = gram(a_bf)
         local_gb = gram(b_bf)
         gram_a, gram_b = lax.psum((local_ga, local_gb), ("row", "col"))

time: 793 us -> 734 us (0.926)
  blocking collectives: 183 us -> 110 us
  starting transfers between devices: 0.25 us -> 13.2 us
    all_gather x2 -> x0, blocking collectives: 60.7 us -> none  [shards(): b_range = lax.all_gather(b_bf, 'row', axis=0, tiled=True)]
    all_to_all x0 -> x2, starting transfers between devices: none -> 13 us  [shards(): lax.all_to_all(jnp.stack([mat] * lax.axis_size(mesh_dim), axis=0), mesh_d...]
    all_gather x2, blocking collectives: 122 us -> 110 us  [shards(): a_range = lax.all_gather(a_bf, 'col', axis=0, tiled=True)]
  transfers between devices with their start and end apart: 6 -> 8, of which waited for: 2 -> 2; matrix products, arithmetic and copies ran while one was open for 2% -> 3% of each run, Pallas kernels for 0% -> 0%
where the time goes in v1:
time: 734 us; the launch traced here: 733 us
  waiting for transfers between devices  556 us (76%)
  blocking collectives  110 us (15%)
  matrix products  21.7 us (3%)
  between operations  16 us (2%)
  starting transfers between devices  13.2 us (2%)
    psum x2, waiting for transfers between devices, shards(): gram_a, gram_b = lax.psum((local_ga, local_gb), ('row', 'col'))  555 us
    all_gather x2, blocking collectives, shards(): a_range = lax.all_gather(a_bf, 'col', axis=0, tiled=True)  110 us
  transfers between devices with their start and end apart: 8, of which 2 were waited for; matrix products, arithmetic and copies ran while one was open for 3% of the time, Pallas kernels for 0%

profile of v1, /device:TPU:17, one launch (start us, length us, event | category | flops | bytes accessed | tf_op | source)
XLA Modules:
  0.0 732.6 jit_solution(461252400431646967)
XLA Ops:
  8.0 0.8 convert_bitcast_fusion
  8.8 0.7 stack.4
  9.5 7.1 all-to-all-start
  16.6 0.9 fusion.68
  17.6 0.7 bitcast_convert_fusion
  18.3 59.5 %all_gather.6 = bf16[512,256]{1,0:T(8,128)(2,1)S(1)} all-gather(bf16[16,256]{1,0:T(8,128)(2,1)S(1)} %bitcast_convert_fusion), channel_id=1, replica_groups=mesh['row'=16,'col'=32] {'col'}, dimensions={0}, use_global_device_ids=true | all-gather | bytes 270336 | tf_op jit(solution)/shard_map/all_gather | solution.py:52
  77.8 0.9 fusion.59
  78.8 6.1 while.28
  82.1 1.7 multiply_reduce_fusion.10
  85.0 1.0 copy.16
  86.9 0.6 fusion.64
  87.6 276.8 %all-reduce.7.cloned.1.call-done = (f32[256,256]{1,0:T(8,128)}, f32[256,256]{1,0:T(8,128)}, f32[512,256]{0,1:T(8,128)}) async-done(((f32[256,256]{1,0:T(8,128)}, f32[256,256]{1,0:T(8,128)}, f32[512,256]{0,1:T(8,128)}), (f32[256,256]{1,0:T(8,128)}, f32[256,256]{1,0:T(8,128)}, f32[512,256]{0,1:T(8,128)})) %all-reduce.7.cloned.1.call-update) | async-done | bytes 1048592 | tf_op jit(solution)/shard_map/psum | solution.py:60
  364.4 1.5 abs_reduce_fusion.3
  366.0 1.7 fusion.66
  367.9 1.6 fusion.65
  369.5 0.7 stack.5
  370.2 5.8 all-to-all-start.1
  376.1 0.9 fusion.69
  377.0 1.6 fusion.67
  378.6 50.6 %all_gather.7 = bf16[512,256]{1,0:T(8,128)(2,1)S(1)} all-gather(bf16[16,256]{1,0:T(8,128)(2,1)S(1)} %get-tuple-element.219), channel_id=1, replica_groups=mesh['row'=16,'col'=32] {'col'}, dimensions={0}, use_global_device_ids=true | all-gather | bytes 270336 | tf_op jit(solution)/shard_map/all_gather | solution.py:52
  429.2 0.9 fusion.70
  430.3 6.3 while.29
  431.0 0.7 fusion.96
  433.7 1.7 multiply_reduce_fusion.12
  436.6 1.0 copy.23
  438.3 0.7 reduce-scatter.9.cloned.1.call-update
  439.0 277.7 %all-reduce.5.cloned.1.call-done = (f32[256,256]{1,0:T(8,128)}, f32[256,256]{1,0:T(8,128)}, f32[512,256]{0,1:T(8,128)}) async-done(((f32[256,256]{1,0:T(8,128)}, f32[256,256]{1,0:T(8,128)}, f32[512,256]{0,1:T(8,128)}), (f32[256,256]{1,0:T(8,128)}, f32[256,256]{1,0:T(8,128)}, f32[512,256]{0,1:T(8,128)})) %all-reduce.5.cloned.1.call-update) | async-done | bytes 1048592 | tf_op jit(solution)/shard_map/psum | solution.py:60
  716.7 1.5 abs_reduce_fusion
  718.2 1.4 fusion.30
  719.6 1.0 copy.25
  720.6 2.2 fusion.35
  722.8 2.2 fusion.40
  (78 shorter events, 3.7 us)
Async XLA Ops:
  8.0 69.8 %copy-start.10 = (f32[1,16,256]{2,1,0:T(8,128)S(1)}, f32[1,16,256]{2,1,0:T(8,128)}, u32[]{:S(2)}) copy-start(f32[1,16,256]{2,1,0:T(8,128)} %param.15) | copy-start | bytes 49156
  8.0 69.7 %copy-start.4 = (f32[512,256]{1,0:T(8,128)S(1)}, f32[512,256]{1,0:T(8,128)}, u32[]{:S(2)}) copy-start(f32[512,256]{1,0:T(8,128)} %param.17) | copy-start | bytes 1572868
  9.5 69.3 %all-to-all-start = ((bf16[16,16,256]{2,1,0:T(8,128)(2,1)}), bf16[16,16,256]{2,1,0:T(8,128)(2,1)S(1)}, u32[]{:S(2)}, u32[]{:S(2)}) async-start(bf16[16,16,256]{2,1,0:T(8,128)(2,1)} %stack.4), calls=%async_computation | async-start | bytes 262144 | tf_op jit(solution)/shard_map/all_to_all | solution.py:54
  16.6 347.8 %all-reduce.7.cloned.1.call-start = ((), (), s32[]{:S(2)}) async-start(), calls=%async_computation.11 | async-start | bytes 2097152 | tf_op jit(solution)/shard_map/psum | solution.py:60
  77.7 1.1 copy-start.16
  82.1 1.7 copy-start.13
  85.0 1.1 copy-start.1
  85.0 1.1 copy-start.3
  86.0 0.9 copy-start.12
  86.1 281.8 %reduce-scatter.7.cloned.1.call-start = ((), (), s32[]{:S(2)}) async-start(), calls=%async_computation.7 | async-start | bytes 278528 | tf_op jit(solution)/shard_map/reduce_scatter | solution.py:87
  86.7 290.3 %reduce-scatter.5.cloned.1.call-start = ((), (), s32[]{:S(2)}) async-start(), calls=%async_computation.6 | async-start | bytes 540672 | tf_op jit(solution)/shard_map/reduce_scatter | solution.py:86
  364.4 1.5 copy-start.5
  364.4 1.5 copy-start.6
  364.4 1.5 copy-start.9
  365.9 1.9 copy-start.11
  370.2 60.0 %all-to-all-start.1 = ((bf16[16,16,256]{2,1,0:T(8,128)(2,1)}), bf16[16,16,256]{2,1,0:T(8,128)(2,1)S(1)}, u32[]{:S(2)}, u32[]{:S(2)}) async-start(bf16[16,16,256]{2,1,0:T(8,128)(2,1)} %stack.5), calls=%async_computation.3 | async-start | bytes 262144 | tf_op jit(solution)/shard_map/all_to_all | solution.py:54
  376.0 340.7 %all-reduce.5.cloned.1.call-start = ((), (), s32[]{:S(2)}) async-start(), calls=%async_computation.10 | async-start | bytes 2097152 | tf_op jit(solution)/shard_map/psum | solution.py:60
  433.7 1.7 copy-start.14
  436.6 1.1 copy-start
  436.6 1.1 copy-start.2
  437.7 283.0 %reduce-scatter.11.cloned.1.call-start = ((), (), s32[]{:S(2)}) async-start(), calls=%async_computation.9 | async-start | bytes 278528 | tf_op jit(solution)/shard_map/reduce_scatter | solution.py:87
  438.2 284.6 %reduce-scatter.9.cloned.1.call-start = ((), (), s32[]{:S(2)}) async-start(), calls=%async_computation.8 | async-start | bytes 540672 | tf_op jit(solution)/shard_map/reduce_scatter | solution.py:86
  716.7 1.5 copy-start.7
  716.7 1.5 copy-start.8
  716.7 1.5 copy-start.15
Sparse Core Ops, SparseCore 0:
  86.2 278.1 all-reduce.6
  437.8 278.8 all-reduce.4
Sparse Core Ops, SparseCore 1:
  89.3 68.7 reduce-scatter.6
  162.5 133.7 reduce-scatter.4
  440.9 69.3 reduce-scatter.10
  514.9 134.1 reduce-scatter.8
